TPU v7x, 256 devices: a whole 4x4x8 slice. The times are simulated.
256 devices in a mesh: sample: 64 (over z, y, core), rep: 4 (over x).
Axes of the slice: x: 4, y: 4, z: 8, core: 2. Of those that a mesh axis runs over, the one named last changes fastest.
Arguments:
- tokens: bfloat16 [32768, 128], P(('sample', 'rep')), may hold values from -6 to 6
- cache: bfloat16 [32768, 48, 256], P(('sample', 'rep')), may hold values from -144 to 144
- gain: float32 [128], replicated, may hold values from 0.25 to 1.75
- w_query: bfloat16 [128, 128], replicated, may hold values from -0.5 to 0.5
- w_key: bfloat16 [128, 128], replicated, may hold values from -0.5 to 0.5
- w_value: bfloat16 [128, 128], replicated, may hold values from -0.5 to 0.5
- w_out: bfloat16 [128, 128], replicated, may hold values from -0.5 to 0.5
- w_head: bfloat16 [128, 4], replicated, may hold values from -0.5 to 0.5
- coef: float32 [32768], P(('sample', 'rep')), may hold values from -0.625 to 0.625
- chosen: int32 [32768], P(('sample', 'rep')), may hold values from 0 to 3
- dest: int32 [32768, 1], P(('sample', 'rep')), may hold values from 0 to 63; in each aligned block of 128 rows (0 to 127, 128 to 255, ...) at most 4 rows name the same one
Outputs:
- new_cache: bfloat16 [65536, 49, 256], P(('sample', 'rep'))
- log_probs: float32 [65536, 4], P(('sample', 'rep'))
- grad_out: float32 [128, 128], replicated
- grad_head: float32 [128, 4], replicated
Inputs may be any that keep to these rules, and one draw needn't show every extreme that they name: `dest`: within the rows of one device, no value is named by more than 4 rows, a bound that some block reaches.
All inputs are finite; a program needn't handle non-finite values.
Results may differ from a plain program's by a relative error of at most 0.022.
Values may be sent and summed in bfloat16 or wider, within the bound.
No kernel may reach another device: no remote copies, remote signals or barrier semaphores. Data moves between devices by JAX's collectives and lax.ppermute only.
A program may use at most 64 MiB of HBM per device.

v0:
```python
import math
import jax
import jax.numpy as jnp
from jax import lax
from jax.sharding import PartitionSpec as P

HEADS = 4
OUTCOMES = 4


def decode_rows(tokens, cache, coef, chosen, gain, w_query, w_key, w_value, w_out, w_head):
    count = tokens.shape[0]
    width = tokens.shape[1]
    levels = cache.shape[1]
    size = width // HEADS
    xf = tokens.astype(jnp.float32)
    normed = (xf * lax.rsqrt(jnp.mean(xf * xf, -1, keepdims=True) + 1e-05) * gain).astype(
        jnp.bfloat16
    )
    query = (
        jnp.dot(normed, w_query, preferred_element_type=jnp.float32) * (1.0 / math.sqrt(size))
    ).astype(jnp.bfloat16)
    key_new = jnp.dot(normed, w_key, preferred_element_type=jnp.float32).astype(jnp.bfloat16)
    value_new = jnp.dot(normed, w_value, preferred_element_type=jnp.float32).astype(jnp.bfloat16)
    query_heads = query.reshape(count, HEADS, size)
    key_rows = cache[:, :, :width].reshape(count, levels, HEADS, size)
    value_rows = cache[:, :, width:].reshape(count, levels, HEADS, size)
    cached_scores = jnp.einsum(
        "yfn,yjfn->yfj", query_heads, key_rows, preferred_element_type=jnp.float32
    )
    score_self = jnp.sum(
        query_heads.astype(jnp.float32) * key_new.astype(jnp.float32).reshape(count, HEADS, size),
        -1,
    )
    top = jnp.maximum(jnp.max(cached_scores, -1), score_self)
    exp_cache = jnp.exp(cached_scores - top[..., None])
    exp_self = jnp.exp(score_self - top)
    total = jnp.sum(exp_cache, -1) + exp_self
    cached_weights = (exp_cache / total[..., None]).astype(jnp.bfloat16)
    weight_self = (exp_self / total).astype(jnp.bfloat16)
    attention_output = jnp.einsum(
        "jat,jtaf->jaf", cached_weights, value_rows, preferred_element_type=jnp.float32
    )
    attention_output = attention_output + weight_self.astype(jnp.float32)[
        ..., None
    ] * value_new.astype(jnp.float32).reshape(count, HEADS, size)
    attention_output = attention_output.reshape(count, width).astype(jnp.bfloat16)
    hidden = (xf + jnp.dot(attention_output, w_out, preferred_element_type=jnp.float32)).astype(
        jnp.bfloat16
    )
    logits = jnp.dot(hidden, w_head, preferred_element_type=jnp.float32)
    logp = jax.nn.log_softmax(logits, -1)
    picked = (chosen[:, None] == jnp.arange(OUTCOMES, dtype=jnp.int32)[None, :]).astype(jnp.float32)
    dlog = coef[:, None] * (picked - jnp.exp(logp))
    grad_head = jnp.dot(hidden.astype(jnp.float32).T, dlog, precision=lax.Precision.HIGHEST)
    hidden_gradient = jnp.dot(dlog, w_head.astype(jnp.float32).T, precision=lax.Precision.HIGHEST)
    grad_out = jnp.dot(
        attention_output.astype(jnp.float32).T, hidden_gradient, precision=lax.Precision.HIGHEST
    )
    both = jnp.concatenate([key_new, value_new], -1)
    return (both, logp, grad_out, grad_head)


def placed(value_rows, place, slots):
    return jnp.zeros((slots,) + value_rows.shape[1:], value_rows.dtype).at[place].set(value_rows)


def on_device(tokens, cache, gain, w_query, w_key, w_value, w_out, w_head, coef, chosen, dest):
    count = tokens.shape[0]
    peers = lax.axis_size("sample")
    capacity = 2 * count // peers
    slots = peers * capacity
    target = dest[:, 0]
    onehot = (target[:, None] == jnp.arange(peers, dtype=jnp.int32)[None, :]).astype(jnp.int32)
    rank = jnp.sum(jnp.cumsum(onehot, 0) * onehot, 1) - 1
    place = target * capacity + rank
    filled = jnp.ones((count,), jnp.int32)
    got_tokens, got_cache, got_coef, got_chosen, got_filled = (
        lax.all_to_all(
            placed(tokens, place, slots), "sample", split_axis=0, concat_axis=0, tiled=True
        ),
        lax.all_to_all(
            placed(cache, place, slots), "sample", split_axis=0, concat_axis=0, tiled=True
        ),
        lax.all_to_all(
            placed(coef, place, slots).astype(jnp.bfloat16),
            "sample",
            split_axis=0,
            concat_axis=0,
            tiled=True,
        ).astype(jnp.float32),
        lax.all_to_all(
            placed(chosen, place, slots), "sample", split_axis=0, concat_axis=0, tiled=True
        ),
        lax.all_to_all(
            placed(filled, place, slots), "sample", split_axis=0, concat_axis=0, tiled=True
        ),
    )
    both, logp, grad_out, grad_head = decode_rows(
        got_tokens, got_cache, got_coef, got_chosen, gain, w_query, w_key, w_value, w_out, w_head
    )
    logp = logp * got_filled[:, None].astype(jnp.float32)
    new_cache = jnp.concatenate([got_cache, both[:, None, :]], 1)
    grad_out, grad_head = lax.psum((grad_out, grad_head), ("sample", "rep"))
    return (new_cache, logp, grad_out, grad_head)


def solution(mesh):
    placed = (
        P(("sample", "rep"), None),
        P(("sample", "rep"), None, None),
        P(),
        P(),
        P(),
        P(),
        P(),
        P(),
        P(("sample", "rep")),
        P(("sample", "rep")),
        P(("sample", "rep"), None),
    )
    return jax.shard_map(
        on_device,
        mesh=mesh,
        in_specs=placed,
        out_specs=(P(("sample", "rep"), None, None), P(("sample", "rep"), None), P(), P()),
        check_vma=False,
    )
```

profile of v0, /device:TPU:1, one launch (start us, length us, event | category | flops | bytes accessed | tf_op | source)
XLA Modules:
  0.0 504.9 jit_solution(15651331253304061399)
XLA Ops:
  7.2 0.0 copy-start
  7.2 0.0 copy-start.1
  7.2 0.9 fusion.8
  8.1 0.2 reduce_window_sum.11
  8.3 0.8 select_reduce_fusion
  9.1 0.7 fusion.13
  9.8 1.1 scatter_custom_fusion.3
  10.9 0.7 all_to_all.36
  11.6 13.2 %all-to-all-start.3 = ((bf16[64,4,1]{1,2,0:T(2,128)(2,1)}), bf16[64,4,1]{1,2,0:T(2,128)(2,1)S(1)}, u32[]{:S(2)}, u32[]{:S(2)}) async-start(bf16[64,4,1]{1,2,0:T(2,128)(2,1)} %all_to_all.36), calls=%async_computation.3 | async-start | bytes 65536 | tf_op jit(solution)/shard_map/all_to_all | solution.py:85
  24.8 1.1 scatter_custom_fusion.4
  25.9 0.7 all_to_all.34
  26.6 7.5 %all-to-all-done.3 = bf16[64,4,1]{1,2,0:T(2,128)(2,1)S(1)} async-done(((bf16[64,4,1]{1,2,0:T(2,128)(2,1)}), bf16[64,4,1]{1,2,0:T(2,128)(2,1)S(1)}, u32[]{:S(2)}, u32[]{:S(2)}) %all-to-all-start.3) | async-done | bytes 544 | tf_op jit(solution)/shard_map/all_to_all | solution.py:85
  34.1 4.7 all-to-all-start.4
  38.8 1.0 scatter_custom_fusion.2
  39.8 0.7 all_to_all.30
  40.5 7.7 %all-to-all-done.4 = s32[64,4,1]{1,2,0:T(1,128)S(1)} async-done(((s32[64,4,1]{1,2,0:T(1,128)}), s32[64,4,1]{1,2,0:T(1,128)S(1)}, u32[]{:S(2)}, u32[]{:S(2)}) %all-to-all-start.4) | async-done | bytes 1056 | tf_op jit(solution)/shard_map/all_to_all | solution.py:92
  48.2 4.7 all-to-all-start.2
  52.9 1.7 scatter_custom_fusion.1
  54.6 7.7 %all-to-all-done.2 = s32[64,4,1]{1,2,0:T(1,128)S(1)} async-done(((s32[64,4,1]{1,2,0:T(1,128)}), s32[64,4,1]{1,2,0:T(1,128)S(1)}, u32[]{:S(2)}, u32[]{:S(2)}) %all-to-all-start.2) | async-done | bytes 1056 | tf_op jit(solution)/shard_map/all_to_all | solution.py:95
  62.3 4.7 all-to-all-start.1
  67.1 3.1 broadcast_in_dim.10
  70.2 16.2 %scatter_fusion = bf16[256,48,256]{2,1,0:T(8,128)(2,1)} fusion(bf16[256,48,256]{2,1,0:T(8,128)(2,1)} %broadcast_in_dim.10, s32[128]{0:T(128)S(1)} %fusion.13, bf16[128,48,256]{2,1,0:T(8,128)(2,1)S(1)} %copy-done.1), kind=kCustom, calls=%fused_computation | custom fusion | bytes 9437696 | tf_op jit(solution)/shard_map/scatter | solution.py:65
  86.4 0.0 all-to-all-done.1
  86.4 10.7 %all-to-all-start = ((bf16[256,48,256]{2,1,0:T(8,128)(2,1)}), bf16[256,48,256]{2,1,0:T(8,128)(2,1)}, u32[]{:S(2)}, u32[]{:S(2)}) async-start(bf16[256,48,256]{2,1,0:T(8,128)(2,1)} %scatter_fusion), calls=%async_computation | async-start | bytes 12582912 | tf_op jit(solution)/shard_map/all_to_all | solution.py:82
  97.1 0.2 all-reduce.2.cloned.1.call-start
  97.3 0.1 convert_reduce_fusion
  97.4 0.1 reshape.124
  97.5 0.5 broadcast.74
  98.0 0.7 reduce.16
  98.8 0.1 eq.34
  98.9 0.1 convert_reduce_fusion.1
  99.0 0.7 convert_element_type.101
  99.6 0.1 multiply_reduce_fusion.2
  99.8 0.1 rsqrt.12
  99.9 0.0 copy-done.7
  99.9 0.7 multiply_convert_fusion
  100.6 0.2 convolution_convert_fusion.1
  100.8 0.2 convolution_convert_fusion
  101.1 0.9 copy.34
  101.9 0.9 bitcast_convert_fusion
  102.8 132.8 %all-to-all-done = bf16[256,48,256]{2,1,0:T(8,128)(2,1)} async-done(((bf16[256,48,256]{2,1,0:T(8,128)(2,1)}), bf16[256,48,256]{2,1,0:T(8,128)(2,1)}, u32[]{:S(2)}, u32[]{:S(2)}) %all-to-all-start) | async-done | bytes 6291488 | tf_op jit(solution)/shard_map/all_to_all | solution.py:82
  235.6 6.7 %fusion.22 = (bf16[256,48,128]{2,1,0:T(8,128)(2,1)}, bf16[256,48,128]{2,1,0:T(8,128)(2,1)}) fusion(bf16[256,48,256]{2,1,0:T(8,128)(2,1)} %all-to-all-done), kind=kLoop, calls=%fused_computation.55 | loop fusion | bytes 12582912 | tf_op jit(solution)/shard_map/slice | solution.py:26
  242.3 3.9 copy.54
  246.2 2.3 multiply_reduce_fusion.1
  248.4 0.0 copy-start.5
  248.5 0.1 reduce_max.19
  248.5 0.1 fusion.3
  248.6 0.1 fusion.7
  248.7 0.8 copy.58
  249.5 3.9 copy.55
  253.4 1.7 multiply_reduce_fusion
  255.1 1.1 fusion.1
  256.2 0.8 fusion.23
  257.1 0.1 fusion.20
  257.3 1.0 fusion.21
  258.3 0.8 fusion.24
  259.1 0.0 all-reduce.2.cloned.1.call-update
  259.1 0.0 copy-start.6
  259.1 3.5 pad_maximum_fusion
  262.7 0.6 subtract_multiply_fusion.1
  263.3 4.3 copy.40
  267.6 78.6 %psum.15 = f32[128,4]{0,1:T(4,128)} all-reduce(f32[128,4]{0,1:T(4,128)S(1)} %fusion.20), channel_id=1, replica_groups=mesh['sample'=64,'rep'=4] {'sample','rep'}, use_global_device_ids=true, to_apply=%region_14.15 | all-reduce | flops 512 | bytes 4096 | tf_op jit(solution)/shard_map/psum | solution.py:104
  346.1 150.5 %all-reduce.2.cloned.1.call-done = f32[128,128]{1,0:T(8,128)} async-done(((f32[128,128]{1,0:T(8,128)}), f32[128,128]{1,0:T(8,128)}) %all-reduce.2.cloned.1.call-update) | async-done | bytes 65552 | tf_op jit(solution)/shard_map/psum | solution.py:104
  496.6 1.5 copy.71
  (21 shorter events, 0.2 us)
Async XLA Ops:
  7.2 94.8 %copy-start = (bf16[128,128]{1,0:T(8,128)(2,1)S(1)}, bf16[128,128]{1,0:T(8,128)(2,1)}, u32[]{:S(2)}) copy-start(bf16[128,128]{1,0:T(8,128)(2,1)} %param.14) | copy-start | bytes 98308
  7.2 63.0 %copy-start.1 = (bf16[128,48,256]{2,1,0:T(8,128)(2,1)S(1)}, bf16[128,48,256]{2,1,0:T(8,128)(2,1)}, u32[]{:S(2)}) copy-start(bf16[128,48,256]{2,1,0:T(8,128)(2,1)} %param.12) | copy-start | bytes 9437188
  11.6 22.5 %all-to-all-start.3 = ((bf16[64,4,1]{1,2,0:T(2,128)(2,1)}), bf16[64,4,1]{1,2,0:T(2,128)(2,1)S(1)}, u32[]{:S(2)}, u32[]{:S(2)}) async-start(bf16[64,4,1]{1,2,0:T(2,128)(2,1)} %all_to_all.36), calls=%async_computation.3 | async-start | bytes 65536 | tf_op jit(solution)/shard_map/all_to_all | solution.py:85
  34.1 14.1 %all-to-all-start.4 = ((s32[64,4,1]{1,2,0:T(1,128)}), s32[64,4,1]{1,2,0:T(1,128)S(1)}, u32[]{:S(2)}, u32[]{:S(2)}) async-start(s32[64,4,1]{1,2,0:T(1,128)} %bitcast.19), calls=%async_computation.4 | async-start | bytes 65536 | tf_op jit(solution)/shard_map/all_to_all | solution.py:92
  48.2 14.1 %all-to-all-start.2 = ((s32[64,4,1]{1,2,0:T(1,128)}), s32[64,4,1]{1,2,0:T(1,128)S(1)}, u32[]{:S(2)}, u32[]{:S(2)}) async-start(s32[64,4,1]{1,2,0:T(1,128)} %bitcast.18), calls=%async_computation.2 | async-start | bytes 65536 | tf_op jit(solution)/shard_map/all_to_all | solution.py:95
  62.3 24.0 %all-to-all-start.1 = ((bf16[64,4,128]{2,1,0:T(4,128)(2,1)}), bf16[64,4,128]{2,1,0:T(4,128)(2,1)S(1)}, u32[]{:S(2)}, u32[]{:S(2)}) async-start(bf16[64,4,128]{2,1,0:T(4,128)(2,1)} %bitcast.5), calls=%async_computation.1 | async-start | bytes 131072 | tf_op jit(solution)/shard_map/all_to_all | solution.py:79
  86.4 13.6 %copy-start.7 = (f32[128]{0:T(128)S(1)}, f32[128]{0:T(128)}, u32[]{:S(2)}) copy-start(f32[128]{0:T(128)} %param.13) | copy-start | bytes 1540
  86.4 14.2 %copy-start.3 = (bf16[128,128]{1,0:T(8,128)(2,1)S(1)}, bf16[128,128]{1,0:T(8,128)(2,1)}, u32[]{:S(2)}) copy-start(bf16[128,128]{1,0:T(8,128)(2,1)} %param.15) | copy-start | bytes 98308
  86.4 14.5 %copy-start.4 = (bf16[128,128]{1,0:T(8,128)(2,1)S(1)}, bf16[128,128]{1,0:T(8,128)(2,1)}, u32[]{:S(2)}) copy-start(bf16[128,128]{1,0:T(8,128)(2,1)} %param.16) | copy-start | bytes 98308
  86.4 149.3 %all-to-all-start = ((bf16[256,48,256]{2,1,0:T(8,128)(2,1)}), bf16[256,48,256]{2,1,0:T(8,128)(2,1)}, u32[]{:S(2)}, u32[]{:S(2)}) async-start(bf16[256,48,256]{2,1,0:T(8,128)(2,1)} %scatter_fusion), calls=%async_computation | async-start | bytes 12582912 | tf_op jit(solution)/shard_map/all_to_all | solution.py:82
  97.1 399.5 %all-reduce.2.cloned.1.call-start = ((), (), s32[]{:S(2)}) async-start(), calls=%async_computation.5 | async-start | bytes 131072 | tf_op jit(solution)/shard_map/psum | solution.py:104
  248.4 6.7 %copy-start.5 = (bf16[128,128]{1,0:T(8,128)(2,1)S(1)}, bf16[128,128]{1,0:T(8,128)(2,1)}, u32[]{:S(2)}) copy-start(bf16[128,128]{1,0:T(8,128)(2,1)} %param.17) | copy-start | bytes 98308
  248.4 10.7 %copy-start.2 = (bf16[256,1,256]{2,1,0:T(2,128)(2,1)S(1)}, bf16[256,1,256]{2,1,0:T(2,128)(2,1)}, u32[]{:S(2)}) copy-start(bf16[256,1,256]{2,1,0:T(2,128)(2,1)} %copy.34) | copy-start | bytes 393220
  259.1 3.5 copy-start.6
Sparse Core Ops, SparseCore 0:
  259.2 237.2 all-reduce.1
where the time goes:
time: 506 us; the launch traced here: 505 us
  waiting for transfers between devices  306 us (60%)
  blocking collectives  78.6 us (16%)
  local copies, waits for them, and re-layouts  49.7 us (10%)
  starting transfers between devices  38.2 us (8%)
  between operations  14.4 us (3%)
  other arithmetic  12.7 us (3%)
  matrix products  5.2 us (1%)
    psum x1, waiting for transfers between devices, on_device(): grad_out, grad_head = lax.psum((grad_out, grad_head), ('sample', 'rep'))  150 us
    all_to_all x1, waiting for transfers between devices, on_device(): lax.all_to_all(placed(cache, place, slots), 'sample', split_axis=0, conca...  133 us
    psum x1, blocking collectives, on_device(): grad_out, grad_head = lax.psum((grad_out, grad_head), ('sample', 'rep'))  78.6 us
    scatter x5, local copies, waits for them, and re-layouts, placed(): jnp.zeros((slots,) + value_rows.shape[1:], value_rows.dtype).at[place]  21.1 us
    unnamed x21, local copies, waits for them, and re-layouts  14.4 us
    all_to_all x1, starting transfers between devices, on_device(): lax.all_to_all(placed(coef, place, slots).astype(jnp.bfloat16), 'sample',...  13.2 us
    all_to_all x1, starting transfers between devices, on_device(): lax.all_to_all(placed(cache, place, slots), 'sample', split_axis=0, conca...  10.7 us
  transfers between devices with their start and end apart: 6, of which 5 were waited for; matrix products, arithmetic and copies ran while one was open for 7% of the time, Pallas kernels for 0%

commit v1 on v0

--- a/solution.py
+++ b/solution.py
@@ -101,7 +101,7 @@
     )
     logp = logp * got_filled[:, None].astype(jnp.float32)
     new_cache = jnp.concatenate([got_cache, both[:, None, :]], 1)
-    grad_out, grad_head = lax.psum((grad_out, grad_head), ("sample", "rep"))
+    grad_out, grad_head = lax.psum(lax.psum((grad_out, grad_head), "rep"), "sample")
     return (new_cache, logp, grad_out, grad_head)
 
 

time: 506 us -> 483 us (0.955)
  waiting for transfers between devices: 306 us -> 222 us
  blocking collectives: 78.6 us -> 136 us
    psum x1 -> x2, waiting for transfers between devices: 150 us -> 66 us  [the longest x1 36.2 us: on_device(): lax.psum((grad_out, grad_head), 'rep')]
    psum x1 -> x2, blocking collectives: 78.6 us -> 136 us  [the longest x1 129 us: on_device(): lax.psum(lax.psum((grad_out, grad_head), 'rep'), 'sample')]
    unnamed x21 -> x19, local copies, waits for them, and re-layouts: 14.4 us -> 16.8 us
  transfers between devices with their start and end apart: 6 -> 7, of which waited for: 5 -> 6; matrix products, arithmetic and copies ran while one was open for 7% -> 9% of each run, Pallas kernels for 0% -> 0%
where the time goes in v1:
time: 483 us; the launch traced here: 482 us
  waiting for transfers between devices  222 us (46%)
  blocking collectives  136 us (28%)
  local copies, waits for them, and re-layouts  51.6 us (11%)
  starting transfers between devices  38.3 us (8%)
  other arithmetic  14.9 us (3%)
  between operations  14.4 us (3%)
    all_to_all x1, waiting for transfers between devices, on_device(): lax.all_to_all(placed(cache, place, slots), 'sample', split_axis=0, conca...  133 us
    psum x1, blocking collectives, on_device(): lax.psum(lax.psum((grad_out, grad_head), 'rep'), 'sample')  129 us
    psum x1, waiting for transfers between devices, on_device(): lax.psum((grad_out, grad_head), 'rep')  36.2 us
    psum x1, waiting for transfers between devices, on_device(): lax.psum(lax.psum((grad_out, grad_head), 'rep'), 'sample')  29.7 us
    scatter x5, local copies, waits for them, and re-layouts, placed(): jnp.zeros((slots,) + value_rows.shape[1:], value_rows.dtype).at[place]  21.1 us
    unnamed x19, local copies, waits for them, and re-layouts  16.8 us
    all_to_all x1, starting transfers between devices, on_device(): lax.all_to_all(placed(coef, place, slots).astype(jnp.bfloat16), 'sample',...  13.2 us
    all_to_all x1, starting transfers between devices, on_device(): lax.all_to_all(placed(cache, place, slots), 'sample', split_axis=0, conca...  10.7 us
  transfers between devices with their start and end apart: 7, of which 6 were waited for; matrix products, arithmetic and copies ran while one was open for 9% of the time, Pallas kernels for 0%

profile of v1, /device:TPU:1, one launch (start us, length us, event | category | flops | bytes accessed | tf_op | source)
XLA Modules:
  0.0 481.6 jit_solution(409296845481508)
XLA Ops:
  7.2 0.0 copy-start
  7.2 0.9 fusion.8
  8.1 0.2 reduce_window_sum.11
  8.3 0.8 select_reduce_fusion
  9.1 0.7 fusion.13
  9.8 1.1 scatter_custom_fusion.3
  10.9 0.7 all_to_all.36
  11.6 13.2 %all-to-all-start.3 = ((bf16[64,4,1]{1,2,0:T(2,128)(2,1)}), bf16[64,4,1]{1,2,0:T(2,128)(2,1)S(1)}, u32[]{:S(2)}, u32[]{:S(2)}) async-start(bf16[64,4,1]{1,2,0:T(2,128)(2,1)} %all_to_all.36), calls=%async_computation.3 | async-start | bytes 65536 | tf_op jit(solution)/shard_map/all_to_all | solution.py:85
  24.8 1.1 scatter_custom_fusion.4
  25.9 0.7 all_to_all.34
  26.6 7.5 %all-to-all-done.3 = bf16[64,4,1]{1,2,0:T(2,128)(2,1)S(1)} async-done(((bf16[64,4,1]{1,2,0:T(2,128)(2,1)}), bf16[64,4,1]{1,2,0:T(2,128)(2,1)S(1)}, u32[]{:S(2)}, u32[]{:S(2)}) %all-to-all-start.3) | async-done | bytes 544 | tf_op jit(solution)/shard_map/all_to_all | solution.py:85
  34.1 4.7 all-to-all-start.4
  38.8 1.0 scatter_custom_fusion.2
  39.8 0.7 all_to_all.30
  40.5 7.7 %all-to-all-done.4 = s32[64,4,1]{1,2,0:T(1,128)S(1)} async-done(((s32[64,4,1]{1,2,0:T(1,128)}), s32[64,4,1]{1,2,0:T(1,128)S(1)}, u32[]{:S(2)}, u32[]{:S(2)}) %all-to-all-start.4) | async-done | bytes 1056 | tf_op jit(solution)/shard_map/all_to_all | solution.py:92
  48.2 4.7 all-to-all-start.2
  52.9 1.7 scatter_custom_fusion.1
  54.6 7.7 %all-to-all-done.2 = s32[64,4,1]{1,2,0:T(1,128)S(1)} async-done(((s32[64,4,1]{1,2,0:T(1,128)}), s32[64,4,1]{1,2,0:T(1,128)S(1)}, u32[]{:S(2)}, u32[]{:S(2)}) %all-to-all-start.2) | async-done | bytes 1056 | tf_op jit(solution)/shard_map/all_to_all | solution.py:95
  62.3 4.7 all-to-all-start.1
  67.1 3.1 broadcast_in_dim.10
  70.2 16.2 %scatter_fusion = bf16[256,48,256]{2,1,0:T(8,128)(2,1)} fusion(bf16[256,48,256]{2,1,0:T(8,128)(2,1)} %broadcast_in_dim.10, s32[128]{0:T(128)S(1)} %fusion.13, bf16[128,48,256]{2,1,0:T(8,128)(2,1)S(1)} %copy-done.1), kind=kCustom, calls=%fused_computation | custom fusion | bytes 9437696 | tf_op jit(solution)/shard_map/scatter | solution.py:65
  86.4 10.7 %all-to-all-start = ((bf16[256,48,256]{2,1,0:T(8,128)(2,1)}), bf16[256,48,256]{2,1,0:T(8,128)(2,1)}, u32[]{:S(2)}, u32[]{:S(2)}) async-start(bf16[256,48,256]{2,1,0:T(8,128)(2,1)} %scatter_fusion), calls=%async_computation | async-start | bytes 12582912 | tf_op jit(solution)/shard_map/all_to_all | solution.py:82
  97.1 0.2 all-reduce.3.cloned.1.call-start
  97.3 0.1 convert_reduce_fusion
  97.4 0.1 reshape.124
  97.5 0.5 broadcast.74
  98.0 0.7 reduce.16
  98.8 0.1 eq.34
  98.9 0.1 convert_reduce_fusion.1
  99.0 0.1 convert_element_type.101
  99.1 0.1 multiply_reduce_fusion.2
  99.3 0.1 rsqrt.12
  99.4 0.7 multiply_convert_fusion
  100.0 0.2 convolution_convert_fusion.1
  100.3 0.2 convolution_convert_fusion
  100.5 0.9 copy.34
  101.4 0.9 bitcast_convert_fusion
  102.2 133.4 %all-to-all-done = bf16[256,48,256]{2,1,0:T(8,128)(2,1)} async-done(((bf16[256,48,256]{2,1,0:T(8,128)(2,1)}), bf16[256,48,256]{2,1,0:T(8,128)(2,1)}, u32[]{:S(2)}, u32[]{:S(2)}) %all-to-all-start) | async-done | bytes 6291488 | tf_op jit(solution)/shard_map/all_to_all | solution.py:82
  235.6 6.6 %fusion.22 = (bf16[256,48,128]{2,1,0:T(8,128)(2,1)}, bf16[256,48,128]{2,1,0:T(8,128)(2,1)}) fusion(bf16[256,48,256]{2,1,0:T(8,128)(2,1)} %all-to-all-done), kind=kLoop, calls=%fused_computation.55 | loop fusion | bytes 12582912 | tf_op jit(solution)/shard_map/slice | solution.py:26
  242.2 3.9 copy.54
  246.1 2.3 multiply_reduce_fusion.1
  248.4 0.0 copy-start.4
  248.4 0.1 reduce_max.19
  248.5 0.1 fusion.3
  248.6 0.1 fusion.7
  248.6 0.1 copy.58
  248.8 3.9 copy.55
  252.7 0.9 multiply_reduce_fusion
  253.6 1.1 fusion.1
  254.7 0.2 fusion.23
  254.9 0.3 fusion.21
  255.3 0.8 fusion.24
  256.1 0.0 all-reduce.3.cloned.1.call-update
  256.1 0.0 all-reduce.5.cloned.1.call-start
  256.2 6.6 %pad_maximum_fusion = bf16[256,49,256]{2,1,0:T(8,128)(2,1)} fusion(bf16[256,1,256]{2,1,0:T(2,128)(2,1)} %copy.34, bf16[256,48,256]{2,1,0:T(8,128)(2,1)} %all-to-all-done), kind=kLoop, calls=%fused_computation.5 | loop fusion | flops 12845056 | bytes 12845056 | tf_op jit(solution)/shard_map/concatenate | solution.py:103
  262.8 0.1 fusion.20
  262.9 36.2 %all-reduce.3.cloned.1.call-done = f32[128,128]{1,0:T(8,128)} async-done(((f32[128,128]{1,0:T(8,128)}), f32[128,128]{1,0:T(8,128)}) %all-reduce.3.cloned.1.call-update) | async-done | bytes 65552 | tf_op jit(solution)/shard_map/psum | solution.py:104
  299.1 0.0 all-reduce.5.cloned.1.call-update
  299.2 0.6 subtract_multiply_fusion.1
  299.8 7.4 %copy.40 = bf16[256,49,256]{2,0,1:T(8,128)(2,1)} copy(bf16[256,49,256]{2,1,0:T(8,128)(2,1)} %pad_maximum_fusion) | data formatting | bytes 12845056
  307.1 7.4 %psum.30 = f32[128,4]{0,1:T(4,128)S(1)} all-reduce(f32[128,4]{0,1:T(4,128)S(1)} %fusion.20), channel_id=1, replica_groups=mesh['sample'=64,'rep'=4] {'rep'}, use_global_device_ids=true, to_apply=%region_15.16 | all-reduce | flops 512 | bytes 4096 | tf_op jit(solution)/shard_map/psum | solution.py:104
  314.5 129.0 %psum.31 = f32[128,4]{0,1:T(4,128)} all-reduce(f32[128,4]{0,1:T(4,128)S(1)} %psum.30), channel_id=1, replica_groups=mesh['sample'=64,'rep'=4] {'sample'}, use_global_device_ids=true, to_apply=%region_16.17 | all-reduce | flops 512 | bytes 4096 | tf_op jit(solution)/shard_map/psum | solution.py:104
  443.5 29.7 %all-reduce.5.cloned.1.call-done = f32[128,128]{1,0:T(8,128)} async-done(((f32[128,128]{1,0:T(8,128)}), f32[128,128]{1,0:T(8,128)}) %all-reduce.5.cloned.1.call-update) | async-done | bytes 65552 | tf_op jit(solution)/shard_map/psum | solution.py:104
  473.3 1.5 copy.72
  (23 shorter events, 0.2 us)
Async XLA Ops:
  7.2 94.2 %copy-start = (bf16[128,128]{1,0:T(8,128)(2,1)S(1)}, bf16[128,128]{1,0:T(8,128)(2,1)}, u32[]{:S(2)}) copy-start(bf16[128,128]{1,0:T(8,128)(2,1)} %param.14) | copy-start | bytes 98308
  7.2 63.0 %copy-start.1 = (bf16[128,48,256]{2,1,0:T(8,128)(2,1)S(1)}, bf16[128,48,256]{2,1,0:T(8,128)(2,1)}, u32[]{:S(2)}) copy-start(bf16[128,48,256]{2,1,0:T(8,128)(2,1)} %param.12) | copy-start | bytes 9437188
  11.6 22.5 %all-to-all-start.3 = ((bf16[64,4,1]{1,2,0:T(2,128)(2,1)}), bf16[64,4,1]{1,2,0:T(2,128)(2,1)S(1)}, u32[]{:S(2)}, u32[]{:S(2)}) async-start(bf16[64,4,1]{1,2,0:T(2,128)(2,1)} %all_to_all.36), calls=%async_computation.3 | async-start | bytes 65536 | tf_op jit(solution)/shard_map/all_to_all | solution.py:85
  34.1 14.1 %all-to-all-start.4 = ((s32[64,4,1]{1,2,0:T(1,128)}), s32[64,4,1]{1,2,0:T(1,128)S(1)}, u32[]{:S(2)}, u32[]{:S(2)}) async-start(s32[64,4,1]{1,2,0:T(1,128)} %bitcast.19), calls=%async_computation.4 | async-start | bytes 65536 | tf_op jit(solution)/shard_map/all_to_all | solution.py:92
  48.2 14.1 %all-to-all-start.2 = ((s32[64,4,1]{1,2,0:T(1,128)}), s32[64,4,1]{1,2,0:T(1,128)S(1)}, u32[]{:S(2)}, u32[]{:S(2)}) async-start(s32[64,4,1]{1,2,0:T(1,128)} %bitcast.18), calls=%async_computation.2 | async-start | bytes 65536 | tf_op jit(solution)/shard_map/all_to_all | solution.py:95
  62.3 24.0 %all-to-all-start.1 = ((bf16[64,4,128]{2,1,0:T(4,128)(2,1)}), bf16[64,4,128]{2,1,0:T(4,128)(2,1)S(1)}, u32[]{:S(2)}, u32[]{:S(2)}) async-start(bf16[64,4,128]{2,1,0:T(4,128)(2,1)} %bitcast.5), calls=%async_computation.1 | async-start | bytes 131072 | tf_op jit(solution)/shard_map/all_to_all | solution.py:79
  86.4 13.0 %copy-start.6 = (f32[128]{0:T(128)S(1)}, f32[128]{0:T(128)}, u32[]{:S(2)}) copy-start(f32[128]{0:T(128)} %param.13) | copy-start | bytes 1540
  86.4 13.7 %copy-start.2 = (bf16[128,128]{1,0:T(8,128)(2,1)S(1)}, bf16[128,128]{1,0:T(8,128)(2,1)}, u32[]{:S(2)}) copy-start(bf16[128,128]{1,0:T(8,128)(2,1)} %param.15) | copy-start | bytes 98308
  86.4 13.9 %copy-start.3 = (bf16[128,128]{1,0:T(8,128)(2,1)S(1)}, bf16[128,128]{1,0:T(8,128)(2,1)}, u32[]{:S(2)}) copy-start(bf16[128,128]{1,0:T(8,128)(2,1)} %param.16) | copy-start | bytes 98308
  86.4 149.3 %all-to-all-start = ((bf16[256,48,256]{2,1,0:T(8,128)(2,1)}), bf16[256,48,256]{2,1,0:T(8,128)(2,1)}, u32[]{:S(2)}, u32[]{:S(2)}) async-start(bf16[256,48,256]{2,1,0:T(8,128)(2,1)} %scatter_fusion), calls=%async_computation | async-start | bytes 12582912 | tf_op jit(solution)/shard_map/all_to_all | solution.py:82
  97.1 202.0 %all-reduce.3.cloned.1.call-start = ((), (), s32[]{:S(2)}) async-start(), calls=%async_computation.5 | async-start | bytes 131072 | tf_op jit(solution)/shard_map/psum | solution.py:104
  248.4 5.2 %copy-start.4 = (bf16[128,128]{1,0:T(8,128)(2,1)S(1)}, bf16[128,128]{1,0:T(8,128)(2,1)}, u32[]{:S(2)}) copy-start(bf16[128,128]{1,0:T(8,128)(2,1)} %param.17) | copy-start | bytes 98308
  248.4 6.3 %copy-start.5 = (bf16[128,4]{0,1:T(4,128)(2,1)S(1)}, bf16[128,4]{0,1:T(4,128)(2,1)}, u32[]{:S(2)}) copy-start(bf16[128,4]{0,1:T(4,128)(2,1)} %param.18) | copy-start | bytes 3076
  256.1 217.1 %all-reduce.5.cloned.1.call-start = ((), (), s32[]{:S(2)}) async-start(), calls=%async_computation.6 | async-start | bytes 131072 | tf_op jit(solution)/shard_map/psum | solution.py:104
Sparse Core Ops, SparseCore 0:
  256.2 42.8 all-reduce.2
  303.0 170.2 all-reduce.4
